TPU v7x, 32 devices: a whole 2x2x4 slice. The times are simulated.
32 devices in a mesh: dp: 4 (over y, core), code: 8 (over z, x).
Axes of the slice: x: 2, y: 2, z: 4, core: 2. Of those that a mesh axis runs over, the one named last changes fastest.
Arguments:
- cached_keys: bfloat16 [131072, 128], P(('dp', 'code')), may hold values from -128 to 128
- codebook: float32 [65536, 128], P('code'), may hold values from -4 to 4
- block_lists: int32 [256, 6], P(('dp', 'code')), may hold values from 0 to 255, as said below
- counts: int32 [256], P(('dp', 'code')), may hold values from 2 to 6, as said below
Outputs:
- codebook_out: float32 [65536, 128], P('code')
- logsum: float32 [131072], P(('dp', 'code'))
Inputs may be any that keep to these rules, and one draw needn't show every extreme that they name: `block_lists`: within a row the first counts entries are distinct; entries past the count repeat the first. Owner o holds blocks o * (256 / the size of code) onward, consecutively; the key blocks of one device (aligned runs of 8 rows) name at most 1 distinct blocks of one owner, and in every draw one owner has exactly 1 named by every device. `counts`: some key block of every device lists 6 blocks.
All inputs are finite; a program needn't handle non-finite values.
Results may differ from a plain program's by a relative error of at most 0.0007.
Values sent between devices are 32-bit elements; how exact they have to be, the bound alone decides.
A program may use at most 64 MiB of HBM per device.

v0:
```python
import functools
import math

import jax
import jax.numpy as jnp
from jax import lax
from jax.experimental import pallas as pl
from jax.experimental.pallas import tpu as pltpu
from jax.sharding import PartitionSpec as P

CBLK = 256
LIST_MAX = 6
ITERS = 2
MROWS = 8
MESH = pl.DeviceIdType.MESH
VLIMIT = 60 * 1024 * 1024
HELD_BYTES = 16 * 1024 * 1024

VM = pl.BlockSpec(memory_space=pltpu.VMEM)
SM = pl.BlockSpec(memory_space=pltpu.SMEM)
ANY = pl.BlockSpec(memory_space=pl.ANY)


def flip(value, bits):
    out = value
    bit = 1
    while bit <= bits:
        if bits & bit:
            out = out + bit * (1 - 2 * (value // bit % 2))
        bit *= 2
    return out


def remote(src, dst, send, recv, dp, code):
    return pltpu.make_async_remote_copy(
        src_ref=src, dst_ref=dst, send_sem=send, recv_sem=recv,
        device_id=(dp, code), device_id_type=MESH,
    )


def fetch_kernel(
    n_code, want_ref, book_hbm, out_ref, served_ref, asked_ref,
    book, ids, id_send, id_recv, send_sem, recv_sem, book_sem, own_sem, smem_sem,
):
    d = lax.axis_index("dp")
    o = lax.axis_index("code")
    barrier = pltpu.get_barrier_semaphore()
    for k in range(1, n_code):
        pl.semaphore_signal(barrier, inc=1, device_id=(d, flip(o, k)), device_id_type=MESH)
    load = pltpu.make_async_copy(book_hbm, book, book_sem)
    load.start()
    own = pltpu.make_async_copy(want_ref.at[o], asked_ref.at[o], own_sem)
    own.start()
    pl.semaphore_wait(barrier, n_code - 1)
    asks = []
    for k in range(1, n_code):
        peer = flip(o, k)
        copy = remote(
            want_ref.at[peer], asked_ref.at[o], id_send.at[k], id_recv.at[k], d, peer
        )
        copy.start()
        asks.append(copy)
    load.wait()
    copies = []
    for k in range(1, n_code):
        peer = flip(o, k)
        asks[k - 1].wait_recv()
        move = pltpu.make_async_copy(asked_ref.at[peer], ids.at[k], smem_sem.at[k])
        move.start()
        move.wait()
        served_ref[peer] = book[ids[k, 0, 0]]
        copy = remote(
            served_ref.at[peer], out_ref.at[o], send_sem.at[k], recv_sem.at[k], d, peer
        )
        copy.start()
        copies.append(copy)
    own.wait()
    move = pltpu.make_async_copy(asked_ref.at[o], ids.at[0], smem_sem.at[0])
    move.start()
    move.wait()
    block = book[ids[0, 0, 0]]
    served_ref[o] = block
    out_ref[o] = block
    for ask in asks:
        ask.wait_send()
    for copy in copies:
        copy.wait()


def exchange_kernel(n_dp, n_code, reply, *refs):
    if reply:
        (sums_ref, served_ref, asked_ref, con_ref, back_ref, acc, stage,
         a_send, a_recv, y_send, y_recv, c_send, c_recv, own_sem, b_send, b_recv) = refs
    else:
        (sums_ref, con_ref,
         a_send, a_recv, y_send, y_recv, c_send, c_recv, own_sem) = refs
    d = lax.axis_index("dp")
    o = lax.axis_index("code")
    n_y = n_dp // 2
    y = d // 2
    core = d % 2
    mate = y * 2 + 1 - core
    barrier = pltpu.get_barrier_semaphore()
    for k in range(1, n_code):
        pl.semaphore_signal(barrier, inc=1, device_id=(d, flip(o, k)), device_id_type=MESH)
    for j in range(1, n_y):
        pl.semaphore_signal(
            barrier, inc=1, device_id=((y + j) % n_y * 2 + core, o), device_id_type=MESH
        )
    pl.semaphore_signal(barrier, inc=1, device_id=(mate, o), device_id_type=MESH)
    own = pltpu.make_async_copy(sums_ref.at[o], con_ref.at[d * n_code + o], own_sem)
    own.start()
    pl.semaphore_wait(barrier, n_code - 1 + n_y - 1 + 1)

    sends = []
    across = []
    for k in range(1, n_code):
        peer = flip(o, k)
        copy = remote(
            sums_ref.at[peer], con_ref.at[d * n_code + o], a_send.at[k], a_recv.at[k], d, peer
        )
        copy.start()
        across.append(copy)
        sends.append(copy)

    def to_y(k, j):
        row = d * n_code + flip(o, k)
        return remote(
            con_ref.at[row], con_ref.at[row], y_send.at[j, k], y_recv.at[j, k],
            (y + j) % n_y * 2 + core, o,
        )

    def held(k, j):
        return ((y + n_y - j) % n_y * 2 + core) * n_code + flip(o, k)

    def to_mate(k, j):
        row = held(k, j)
        return remote(
            con_ref.at[row], con_ref.at[row], c_send.at[j, k], c_recv.at[j, k], mate, o
        )

    if reply:
        acc[...] = jnp.zeros_like(acc)

    def absorb(row):
        if not reply:
            return
        here = con_ref[row, pl.ds(CBLK + 2, 1), :]

        def one(i, c):
            same = (asked_ref[i, pl.ds(0, 1), :].astype(jnp.float32) == here).astype(jnp.float32)
            acc[i] += con_ref[row] * same
            return c

        lax.fori_loop(0, n_code, one, 0)

    y_copies = {}
    mates = {}
    for k in range(n_code):
        if k == 0:
            own.wait()
        else:
            across[k - 1].wait_recv()
        for j in range(1, n_y):
            copy = to_y(k, j)
            copy.start()
            y_copies[j, k] = copy
            sends.append(copy)
        copy = to_mate(k, 0)
        copy.start()
        mates[0, k] = copy
        sends.append(copy)
        absorb(held(k, 0))
    for k in range(n_code):
        for j in range(1, n_y):
            y_copies[j, k].wait_recv()
            copy = to_mate(k, j)
            copy.start()
            mates[j, k] = copy
            sends.append(copy)
            absorb(held(k, j))
        mates[0, k].wait_recv()
        absorb(held(k, 0) + (1 - 2 * core) * n_code)
    for k in range(n_code):
        for j in range(1, n_y):
            mates[j, k].wait_recv()
            absorb(held(k, j) + (1 - 2 * core) * n_code)
    if reply:
        backs = []
        for k in range(n_code):
            peer = flip(o, k)
            for h in range(2):
                inv = 1.0 / (acc[peer, pl.ds(CBLK + h, 1), :] + 1.0)
                column = jnp.transpose(jnp.broadcast_to(inv, (128, 128)))
                rows = pl.ds(h * 128, 128)
                fresh = (acc[peer, rows, :] + served_ref[peer, rows, :]) * column
                if k == 0:
                    back_ref[o, rows, :] = fresh
                else:
                    stage[k, rows, :] = fresh
        for k in range(n_code - 1, 0, -1):
            copy = remote(
                stage.at[k], back_ref.at[o], b_send.at[k], b_recv.at[k], d, flip(o, k)
            )
            copy.start()
            backs.append(copy)
        for copy in backs:
            copy.wait()
    for copy in sends:
        copy.wait_send()


def fused_kernel(n_dp, n_code, key_blocks, block, feature, reply, *refs):
    slots_ref, counts_ref, fetched_ref, keys_ref, want_ref = refs[:5]
    refs = refs[5:]
    if reply:
        served_ref, asked_ref, con_ref, logsum_ref, back_ref = refs[:5]
        refs = refs[5:]
        acc, stage, b_send, b_recv = refs[:4]
        refs = refs[4:]
    else:
        con_ref, logsum_ref = refs[:2]
        refs = refs[2:]
    (words, norms, kst, kext, scores, post, sums, part,
     a_send, a_recv, y_send, y_recv, c_send, c_recv, own_sem) = refs
    scale = math.log2(math.e) / math.sqrt(feature)
    d = lax.axis_index("dp")
    o = lax.axis_index("code")
    n_y = n_dp // 2
    y = d // 2
    core = d % 2
    mate = y * 2 + 1 - core
    barrier = pltpu.get_barrier_semaphore()
    for k in range(1, n_code):
        pl.semaphore_signal(barrier, inc=1, device_id=(d, flip(o, k)), device_id_type=MESH)
    for j in range(1, n_y):
        pl.semaphore_signal(
            barrier, inc=1, device_id=((y + j) % n_y * 2 + core, o), device_id_type=MESH
        )
    pl.semaphore_signal(barrier, inc=1, device_id=(mate, o), device_id_type=MESH)

    def prepare(s, c):
        value = fetched_ref[s]
        scaled = value * scale
        hi = scaled.astype(jnp.bfloat16)
        words[s, :, 0:128] = hi
        words[s, :, 128:256] = (scaled - hi.astype(jnp.float32)).astype(jnp.bfloat16)
        half = (0.5 * scale) * jnp.sum(value * value, axis=1, keepdims=True)
        norms[s] = jnp.broadcast_to(half, (CBLK, 128))
        return c

    lax.fori_loop(0, n_code, prepare, 0)
    kext[:, 0:128] = keys_ref[...]
    kext[:, 128:256] = jnp.ones((key_blocks * block, 128), jnp.bfloat16)
    post[key_blocks * LIST_MAX] = jnp.zeros((CBLK, block), jnp.bfloat16)

    def key_block(kb, c):
        keys = keys_ref[pl.ds(pl.multiple_of(kb * block, block), block), :]
        turned = jnp.transpose(keys)
        kst[0:128, :] = turned
        kst[128:256, :] = turned
        count = counts_ref[kb]
        slots = [slots_ref[kb, l] for l in range(LIST_MAX)]
        picked = jnp.concatenate([words[slots[l]] for l in range(LIST_MAX)], axis=0)
        raw = jnp.dot(picked, kst[...], preferred_element_type=jnp.float32)
        top = jnp.full((8, block), -3e38, jnp.float32)
        for l in range(LIST_MAX):
            rows = slice(l * CBLK, (l + 1) * CBLK)
            less = norms[slots[l]] + jnp.where(l < count, 0.0, 1e30)
            s = raw[rows] - jnp.tile(less, (1, block // 128))
            scores[rows, :] = s
            top = jnp.maximum(top, jnp.max(s.reshape(CBLK // 8, 8, block), axis=0))
        peak = jnp.max(top, axis=0, keepdims=True)
        total = jnp.zeros((8, block), jnp.float32)
        for l in range(LIST_MAX):
            rows = slice(l * CBLK, (l + 1) * CBLK)
            e = jnp.exp2(scores[rows, :] - peak)
            scores[rows, :] = e
            total = total + jnp.sum(e.reshape(CBLK // 8, 8, block), axis=0)
        total = jnp.sum(total, axis=0, keepdims=True)
        logsum_ref[kb] = peak * math.log(2.0) + jnp.log(total)
        inv = 1.0 / total
        for l in range(LIST_MAX):
            rows = slice(l * CBLK, (l + 1) * CBLK)
            post[kb * LIST_MAX + l] = (scores[rows, :] * inv).astype(jnp.bfloat16)
        return c

    lax.fori_loop(0, key_blocks, key_block, 0)

    def collect(slot):
        for kb in range(key_blocks):
            entry = key_blocks * LIST_MAX
            for l in range(LIST_MAX):
                hit = (slots_ref[kb, l] == slot) & (counts_ref[kb] > l)
                entry = jnp.where(hit, kb * LIST_MAX + l, entry)
            piece = jnp.dot(
                post[entry], kext[kb * block : (kb + 1) * block, :],
                preferred_element_type=jnp.float32,
            )
            if kb == 0:
                part[...] = piece
            else:
                part[...] += piece
        for h in range(2):
            turned = jnp.transpose(part[h * 128 : (h + 1) * 128, 128:256])
            sums[slot, CBLK + h : CBLK + h + 1, :] = turned[0:1, :]
        sums[slot, CBLK + 2 :, :] = want_ref[slot, 2:, :].astype(jnp.float32)
        sums[slot, :CBLK, :] = part[:, 0:128]

    def turn(k):
        out = o
        bit = 1
        while bit < n_code:
            out = out + bit * (k // bit % 2) * (1 - 2 * (o // bit % 2))
            bit *= 2
        return out

    def across(k):
        peer = turn(k)
        return remote(
            sums.at[peer], con_ref.at[d * n_code + o], a_send.at[k], a_recv.at[k], d, peer
        )

    far = n_code // 2
    collect(turn(far))
    pl.semaphore_wait(barrier, n_code - 1 + n_y - 1 + 1)

    def step(k, c):
        collect(turn(k))
        across(k - 1).start()
        return c

    lax.fori_loop(far + 1, n_code, step, 0)
    collect(o)
    across(n_code - 1).start()
    own = pltpu.make_async_copy(sums.at[o], con_ref.at[d * n_code + o], own_sem)
    own.start()

    def held(k, j):
        return ((y + n_y - j) % n_y * 2 + core) * n_code + flip(o, k)

    sends = []

    def to_y(k, j):
        row = held(k, 0)
        copy = remote(
            con_ref.at[row], con_ref.at[row], y_send.at[j, k], y_recv.at[j, k],
            (y + j) % n_y * 2 + core, o,
        )
        copy.start()
        sends.append(copy)
        return copy

    def to_mate(k, j):
        row = held(k, j)
        copy = remote(
            con_ref.at[row], con_ref.at[row], c_send.at[j, k], c_recv.at[j, k], mate, o
        )
        copy.start()
        sends.append(copy)
        return copy

    if reply:
        acc[...] = jnp.zeros_like(acc)

    def absorb(row):
        if not reply:
            return
        here = con_ref[row, pl.ds(CBLK + 2, 1), :]

        def one(i, c):
            same = (asked_ref[i, pl.ds(0, 1), :].astype(jnp.float32) == here).astype(jnp.float32)
            acc[i] += con_ref[row] * same
            return c

        lax.fori_loop(0, n_code, one, 0)

    y_copies = {}
    mates = {}
    own.wait()
    for j in range(1, n_y):
        y_copies[j, 0] = to_y(0, j)
    mates[0, 0] = to_mate(0, 0)

    def near(k, c):
        collect(turn(k))

        @pl.when(k > 1)
        def _():
            across(k - 1).start()

        return c

    lax.fori_loop(1, far, near, 0)
    absorb(held(0, 0))
    across(far - 1).start()

    for k in range(1, n_code):
        across(k).wait_recv()
        for j in range(1, n_y):
            y_copies[j, k] = to_y(k, j)
        mates[0, k] = to_mate(k, 0)
        absorb(held(k, 0))
    for k in range(n_code):
        for j in range(1, n_y):
            y_copies[j, k].wait_recv()
            mates[j, k] = to_mate(k, j)
            absorb(held(k, j))
        mates[0, k].wait_recv()
        absorb(held(k, 0) + (1 - 2 * core) * n_code)
    for k in range(n_code):
        for j in range(1, n_y):
            mates[j, k].wait_recv()
            absorb(held(k, j) + (1 - 2 * core) * n_code)
    if reply:
        order = list(range(far, n_code)) + list(range(1, far))
        for k in order + [0]:
            peer = flip(o, k)
            for h in range(2):
                inv = 1.0 / (acc[peer, pl.ds(CBLK + h, 1), :] + 1.0)
                column = jnp.transpose(jnp.broadcast_to(inv, (128, 128)))
                rows = pl.ds(h * 128, 128)
                fresh = (acc[peer, rows, :] + served_ref[peer, rows, :]) * column
                if k == 0:
                    back_ref[o, rows, :] = fresh
                else:
                    stage[k, rows, :] = fresh
        backs = []
        for k in order:
            copy = remote(
                stage.at[k], back_ref.at[o], b_send.at[k], b_recv.at[k], d, flip(o, k)
            )
            copy.start()
            backs.append(copy)
        for copy in backs:
            copy.wait()
    for k in range(1, n_code):
        across(k).wait_send()
    for copy in sends:
        copy.wait_send()


def finish_kernel(n, own_blocks, sweeps, *refs):
    con_hbm = refs[:sweeps]
    book_hbm, out_hbm = refs[sweeps : sweeps + 2]
    con, total, mass, ids, con_sem, book_sem, out_sem = refs[sweeps + 2 :]
    book = pltpu.make_async_copy(book_hbm, total, book_sem)
    book.start()
    half = n // 2

    def load(t, h):
        rows = pl.ds(h * half, half)
        return pltpu.make_async_copy(con_hbm[t].at[rows], con.at[rows], con_sem.at[h])

    load(0, 0).start()
    load(0, 1).start()
    outs = []
    for t in range(sweeps):
        mass[...] = jnp.ones_like(mass)
        for h in range(2):
            load(t, h).wait()
            if t == 0:

                def name(j, c):
                    for u in range(4):
                        i = j * 4 + u
                        ids[i] = jnp.max(con[i, pl.ds(CBLK + 2, 1), :]).astype(jnp.int32)
                    return c

                lax.fori_loop(h * half // 4, (h + 1) * half // 4, name, 0)
                if h == 0:
                    book.wait()

            def add(j, c):
                b = ids[j]
                total[b] += con[j, :CBLK, :]
                for g in range(2):
                    row = pl.ds(g * (mass.shape[0] // 2) + b, 1)
                    mass[row, :] += con[j, pl.ds(CBLK + g, 1), :]
                return c

            lax.fori_loop(h * half, (h + 1) * half, add, 0)
            if t + 1 < sweeps:
                load(t + 1, h).start()
        columns = jnp.transpose(1.0 / mass[...])
        for b in range(own_blocks):
            for g in range(2):
                lane = g * (mass.shape[0] // 2) + b
                total[b, g * 128 : (g + 1) * 128, :] = (
                    total[b, g * 128 : (g + 1) * 128, :] * columns[:, lane : lane + 1]
                )
            if t + 1 == sweeps:
                out = pltpu.make_async_copy(total.at[b], out_hbm.at[b], out_sem.at[b])
                out.start()
                outs.append(out)
    for out in outs:
        out.wait()


def assign_kernel(
    n_slots, key_blocks, block, feature,
    slots_ref, counts_ref, fetched_ref, keys_ref, want_ref,
    sums_ref, logsum_ref,
    words, norms, kst, kext, picked, scores, post, acc,
):
    scale = math.log2(math.e) / math.sqrt(feature)

    for s in range(n_slots):
        value = fetched_ref[s]
        scaled = value * scale
        hi = scaled.astype(jnp.bfloat16)
        words[s, :, 0:128] = hi
        words[s, :, 128:256] = (scaled - hi.astype(jnp.float32)).astype(jnp.bfloat16)
        half = (0.5 * scale) * jnp.sum(value * value, axis=1, keepdims=True)
        norms[s] = jnp.broadcast_to(half, (CBLK, 128))
        acc[s] = jnp.zeros((CBLK, 256), jnp.float32)
    kext[:, 128:256] = jnp.ones((block, 128), jnp.bfloat16)

    def key_block(kb, c):
        keys = keys_ref[pl.ds(pl.multiple_of(kb * block, block), block), :]
        kext[:, 0:128] = keys
        turned = jnp.transpose(keys)
        kst[0:128, :] = turned
        kst[128:256, :] = turned
        count = counts_ref[kb]
        slots = [slots_ref[kb, l] for l in range(LIST_MAX)]
        for l in range(LIST_MAX):
            picked[l * CBLK : (l + 1) * CBLK, :] = words[slots[l]]
        raw = jnp.dot(picked[...], kst[...], preferred_element_type=jnp.float32)
        top = jnp.full((8, block), -3e38, jnp.float32)
        for l in range(LIST_MAX):
            rows = slice(l * CBLK, (l + 1) * CBLK)
            less = norms[slots[l]] + jnp.where(l < count, 0.0, 1e30)
            s = raw[rows] - jnp.tile(less, (1, block // 128))
            scores[rows, :] = s
            top = jnp.maximum(top, jnp.max(s.reshape(CBLK // 8, 8, block), axis=0))
        peak = jnp.max(top, axis=0, keepdims=True)
        total = jnp.zeros((8, block), jnp.float32)
        for l in range(LIST_MAX):
            rows = slice(l * CBLK, (l + 1) * CBLK)
            e = jnp.exp2(scores[rows, :] - peak)
            scores[rows, :] = e
            total = total + jnp.sum(e.reshape(CBLK // 8, 8, block), axis=0)
        total = jnp.sum(total, axis=0, keepdims=True)
        logsum_ref[kb] = peak * math.log(2.0) + jnp.log(total)
        inv = 1.0 / total
        post[...] = (scores[...] * inv).astype(jnp.bfloat16)
        weighted = jnp.dot(post[...], kext[...], preferred_element_type=jnp.float32)
        for l in range(LIST_MAX):
            acc[slots[l]] += weighted[l * CBLK : (l + 1) * CBLK]
        return c

    lax.fori_loop(0, key_blocks, key_block, 0)

    for s in range(n_slots):
        sums_ref[s, :CBLK, :] = acc[s, :, 0:128]
        for h in range(2):
            turned = jnp.transpose(acc[s, h * 128 : (h + 1) * 128, 128:256])
            sums_ref[s, CBLK + h : CBLK + h + 1, :] = turned[0:1, :]
        sums_ref[s, CBLK + 2 :, :] = want_ref[s, 2:, :].astype(jnp.float32)


def on_device(cached_keys, codebook, block_lists, counts):
    n_dp = lax.axis_size("dp")
    n_code = lax.axis_size("code")
    n = n_dp * n_code
    own_rows, feature = codebook.shape
    own_blocks = own_rows // CBLK
    key_blocks = block_lists.shape[0]
    block = cached_keys.shape[0] // key_blocks
    f32 = jnp.float32
    dma = pltpu.SemaphoreType.DMA

    slots = block_lists // own_blocks
    local = block_lists % own_blocks
    wanted = jnp.max(
        jnp.where(
            slots.reshape(-1)[:, None] == jnp.arange(128)[None, :], local.reshape(-1)[:, None], 0
        ),
        axis=0,
    )
    want = jnp.broadcast_to(wanted[:n_code, None, None], (n_code, 8, 128)).astype(jnp.int32)
    blocks = jax.ShapeDtypeStruct((n_code, CBLK, feature), f32)
    sums_shape = jax.ShapeDtypeStruct((n_code, CBLK + MROWS, feature), f32)
    con_shape = jax.ShapeDtypeStruct((n, CBLK + MROWS, feature), f32)
    n_y = n_dp // 2

    def params(**kw):
        return pltpu.CompilerParams(vmem_limit_bytes=VLIMIT, **kw)

    book = codebook.reshape(own_blocks, CBLK, feature)
    fetched, served, asked = pl.pallas_call(
        functools.partial(fetch_kernel, n_code),
        out_shape=(blocks, blocks, jax.ShapeDtypeStruct((n_code, 8, 128), jnp.int32)),
        in_specs=[VM, ANY],
        out_specs=(VM, VM, VM),
        scratch_shapes=[
            pltpu.VMEM((own_blocks, CBLK, feature), f32),
            pltpu.SMEM((n_code, 8, 128), jnp.int32),
            dma((n_code,)), dma((n_code,)), dma((n_code,)), dma((n_code,)),
            dma, dma, dma((n_code,)),
        ],
        compiler_params=params(collective_id=0, has_side_effects=True),
    )(want, book)
    logsum = None
    gathered = []
    current = book
    joint = ITERS * n * (CBLK + MROWS) * feature * 4 <= HELD_BYTES

    def finish(parts, held):
        return pl.pallas_call(
            functools.partial(finish_kernel, n, own_blocks, len(parts)),
            out_shape=jax.ShapeDtypeStruct((own_blocks, CBLK, feature), f32),
            in_specs=[ANY] * (len(parts) + 1),
            out_specs=ANY,
            scratch_shapes=[
                pltpu.VMEM(con_shape.shape, f32),
                pltpu.VMEM((own_blocks, CBLK, feature), f32),
                pltpu.VMEM((max(128, 2 * own_blocks), 128), f32),
                pltpu.SMEM((n,), jnp.int32),
                dma((2,)), dma, dma((own_blocks,)),
            ],
            compiler_params=params(),
        )(*parts, held)

    for sweep in range(ITERS):
        reply = sweep + 1 < ITERS
        sems = [
            dma((n_code,)), dma((n_code,)),
            dma((n_y, n_code)), dma((n_y, n_code)),
            dma((n_y, n_code)), dma((n_y, n_code)),
            dma,
        ]
        if joint:
            ins = [slots, counts, fetched, cached_keys, want]
            outs = [con_shape, jax.ShapeDtypeStruct((key_blocks, 1, block), f32)]
            scratch = []
            if reply:
                ins += [served, asked]
                outs += [blocks]
                scratch = [
                    pltpu.VMEM(sums_shape.shape, f32), pltpu.VMEM(blocks.shape, f32),
                    dma((n_code,)), dma((n_code,)),
                ]
            scratch += [
                pltpu.VMEM((n_code, CBLK, 256), jnp.bfloat16),
                pltpu.VMEM((n_code, CBLK, 128), f32),
                pltpu.VMEM((256, block), jnp.bfloat16),
                pltpu.VMEM((key_blocks * block, 256), jnp.bfloat16),
                pltpu.VMEM((LIST_MAX * CBLK, block), f32),
                pltpu.VMEM((key_blocks * LIST_MAX + 1, CBLK, block), jnp.bfloat16),
                pltpu.VMEM(sums_shape.shape, f32),
                pltpu.VMEM((CBLK, 256), f32),
            ] + sems
            results = pl.pallas_call(
                functools.partial(
                    fused_kernel, n_dp, n_code, key_blocks, block, feature, reply
                ),
                out_shape=tuple(outs),
                in_specs=[SM, SM] + [VM] * (len(ins) - 2),
                out_specs=(VM,) * len(outs),
                scratch_shapes=scratch,
                compiler_params=params(collective_id=1 + sweep, has_side_effects=True),
            )(*ins)
            con, logsum = results[:2]
            if reply:
                fetched = results[2]
        else:
            sums, logsum = pl.pallas_call(
                functools.partial(assign_kernel, n_code, key_blocks, block, feature),
                out_shape=(sums_shape, jax.ShapeDtypeStruct((key_blocks, 1, block), f32)),
                in_specs=[SM, SM, VM, VM, VM],
                out_specs=(VM, VM),
                scratch_shapes=[
                    pltpu.VMEM((n_code, CBLK, 256), jnp.bfloat16),
                    pltpu.VMEM((n_code, CBLK, 128), f32),
                    pltpu.VMEM((256, block), jnp.bfloat16),
                    pltpu.VMEM((block, 256), jnp.bfloat16),
                    pltpu.VMEM((LIST_MAX * CBLK, 256), jnp.bfloat16),
                    pltpu.VMEM((LIST_MAX * CBLK, block), f32),
                    pltpu.VMEM((LIST_MAX * CBLK, block), jnp.bfloat16),
                    pltpu.VMEM((n_code, CBLK, 256), f32),
                ],
                compiler_params=params(),
            )(slots, counts, fetched, cached_keys, want)
            if reply:
                con, fetched = pl.pallas_call(
                    functools.partial(exchange_kernel, n_dp, n_code, True),
                    out_shape=(con_shape, blocks),
                    in_specs=[VM, VM, VM],
                    out_specs=(VM, VM),
                    scratch_shapes=[
                        pltpu.VMEM(sums_shape.shape, f32), pltpu.VMEM(blocks.shape, f32)
                    ] + sems + [dma((n_code,)), dma((n_code,))],
                    compiler_params=params(collective_id=1 + sweep, has_side_effects=True),
                )(sums, served, asked)
            else:
                con = pl.pallas_call(
                    functools.partial(exchange_kernel, n_dp, n_code, False),
                    out_shape=con_shape,
                    in_specs=[VM],
                    out_specs=VM,
                    scratch_shapes=sems,
                    compiler_params=params(collective_id=1 + sweep, has_side_effects=True),
                )(sums)
        gathered.append(con)
        if not joint:
            current = finish(gathered, current)
            gathered = []
            if reply:
                current, fetched = lax.optimization_barrier((current, fetched))
    if gathered:
        current = finish(gathered, current)
    return (current.reshape(own_rows, feature), logsum.reshape(-1))


def solution(mesh):
    in_specs = (
        P(("dp", "code"), None),
        P("code", None),
        P(("dp", "code"), None),
        P(("dp", "code")),
    )
    out_specs = (P("code", None), P(("dp", "code")))
    return jax.shard_map(
        on_device, mesh=mesh, in_specs=in_specs, out_specs=out_specs, check_vma=False
    )
```

profile of v0, /device:TPU:1, one launch (start us, length us, event | category | flops | bytes accessed | tf_op | source)
XLA Modules:
  0.0 181.2 jit_solution(13391707991883838121)
XLA Ops:
  0.6 0.7 add_select_fusion
  1.3 0.0 copy-start
  1.3 0.1 broadcast_in_dim.21
  1.4 0.1 eq.17
  1.5 0.1 select_reduce_fusion
  1.6 0.7 broadcast_in_dim.24.want_ref.refs_4_
  2.3 27.1 %shard_map.59 = (f32[8,256,128]{2,1,0:T(8,128)}, f32[8,256,128]{2,1,0:T(8,128)}, s32[8,8,128]{2,1,0:T(8,128)}) custom-call(s32[8,8,128]{2,1,0:T(8,128)} %broadcast_in_dim.24.want_ref.refs_4_, f32[32,256,128]{2,1,0:T(8,128)} %bitcast.4), custom_call_target="tpu_custom_call" | custom-call | tf_op jit(solution)/shard_map/pallas_call | solution.py:592
  29.4 0.0 copy-done
  29.4 81.6 %shard_map.60 = (f32[32,264,128]{2,1,0:T(8,128)}, f32[8,1,512]{2,1,0:T(1,128)}, f32[8,256,128]{2,1,0:T(8,128)}) custom-call(s32[8,6]{1,0:T(8,128)} %copy-done, s32[8]{0:T(128)} %refs_1_.3, f32[8,256,128]{2,1,0:T(8,128)} %get-tuple-element.9.refs_2_, bf16[4096,128]{1,0:T(8,128)(2,1)} %refs_3_.3, s32[8,8,128]{2,1,0:T(8,128)} %broadcast_in_dim.24.want_ref.refs_4_, ...), custom_call_target="tpu_custom_call" | custom-call | tf_op jit(solution)/shard_map/pallas_call | solution.py:655
  111.0 60.7 %shard_map.61 = (f32[32,264,128]{2,1,0:T(8,128)}, f32[8,1,512]{2,1,0:T(1,128)}) custom-call(s32[8,6]{1,0:T(8,128)} %copy-done, s32[8]{0:T(128)} %refs_1_.3, f32[8,256,128]{2,1,0:T(8,128)} %get-tuple-element.13.refs_2_, bf16[4096,128]{1,0:T(8,128)(2,1)} %refs_3_.3, s32[8,8,128]{2,1,0:T(8,128)} %broadcast_in_dim.24.want_ref.refs_4_), custom_call_target="tpu_custom_call" | custom-call | tf_op jit(solution)/shard_map/pallas_call | solution.py:655
  171.7 0.0 copy-start.1
  171.7 8.9 %shard_map.62 = f32[32,256,128]{2,1,0:T(8,128)} custom-call(f32[32,264,128]{2,1,0:T(8,128)} %get-tuple-element.12.refs_0_, f32[32,264,128]{2,1,0:T(8,128)} %get-tuple-element.14.refs_1_, f32[32,256,128]{2,1,0:T(8,128)} %bitcast.5), custom_call_target="tpu_custom_call" | custom-call | tf_op jit(solution)/shard_map/pallas_call | solution.py:611
  180.6 0.0 copy-done.1
  180.6 0.6 copy.7
Async XLA Ops:
  1.3 28.0 %copy-start = (s32[8,6]{1,0:T(8,128)}, s32[8,6]{1,0:T(8,128)S(1)}, u32[]{:S(2)}) copy-start(s32[8,6]{1,0:T(8,128)S(1)} %get-tuple-element.17.refs_0_) | copy-start | bytes 580
  171.7 8.9 %copy-start.1 = (f32[8,1,512]{2,1,0:T(1,128)S(1)}, f32[8,1,512]{2,1,0:T(1,128)}, u32[]{:S(2)}) copy-start(f32[8,1,512]{2,1,0:T(1,128)} %get-tuple-element.15) | copy-start | bytes 49156
where the time goes:
time: 182 us; the launch traced here: 181 us
  Pallas kernels  178 us (98%)
    pallas_call x2, Pallas kernels, on_device(): pl.pallas_call(functools.partial(fused_kernel, n_dp, n_code, key_blocks,...  142 us
    pallas_call x1, Pallas kernels, on_device(): pl.pallas_call(functools.partial(fetch_kernel, n_code), out_shape=(blocks...  27.1 us
    pallas_call x1, Pallas kernels, finish(): pl.pallas_call(functools.partial(finish_kernel, n, own_blocks, len(parts)...  8.88 us

commit v1 on v0

--- a/solution.py
+++ b/solution.py
@@ -210,26 +210,34 @@
         copy.wait_send()
 
 
-def fused_kernel(n_dp, n_code, key_blocks, block, feature, reply, *refs):
-    slots_ref, counts_ref, fetched_ref, keys_ref, want_ref = refs[:5]
-    refs = refs[5:]
-    if reply:
-        served_ref, asked_ref, con_ref, logsum_ref, back_ref = refs[:5]
-        refs = refs[5:]
-        acc, stage, b_send, b_recv = refs[:4]
-        refs = refs[4:]
-    else:
-        con_ref, logsum_ref = refs[:2]
-        refs = refs[2:]
-    (words, norms, kst, kext, scores, post, sums, part,
-     a_send, a_recv, y_send, y_recv, c_send, c_recv, own_sem) = refs
+def sweeps_kernel(n_dp, n_code, key_blocks, block, own_blocks, feature, sweeps, *refs):
+    slots_ref, counts_ref, want_ref, keys_ref, book_hbm = refs[:5]
+    con_refs = refs[5 : 5 + sweeps]
+    logsum_ref = refs[5 + sweeps]
+    (unnorm, peaks, totals, words, norms, kst, kext, sums, acc, stage, served,
+     fetched, back, asked, part, less, ids,
+     id_send, id_recv, f_send, f_recv, b_send, b_recv,
+     a_send, a_recv, y_send, y_recv, c_send, c_recv,
+     book_sem, own_sem, smem_sem) = refs[6 + sweeps :]
     scale = math.log2(math.e) / math.sqrt(feature)
+    keys = key_blocks * block
+    chunks = keys // 128
     d = lax.axis_index("dp")
     o = lax.axis_index("code")
     n_y = n_dp // 2
     y = d // 2
     core = d % 2
     mate = y * 2 + 1 - core
+    far = n_code // 2
+
+    def turn(k):
+        out = o
+        bit = 1
+        while bit < n_code:
+            out = out + bit * (k // bit % 2) * (1 - 2 * (o // bit % 2))
+            bit *= 2
+        return out
+
     barrier = pltpu.get_barrier_semaphore()
     for k in range(1, n_code):
         pl.semaphore_signal(barrier, inc=1, device_id=(d, flip(o, k)), device_id_type=MESH)
@@ -239,204 +247,292 @@
         )
     pl.semaphore_signal(barrier, inc=1, device_id=(mate, o), device_id_type=MESH)
 
-    def prepare(s, c):
-        value = fetched_ref[s]
+    book = unnorm.at[n_code - 1]
+    load = pltpu.make_async_copy(book_hbm, book.at[pl.ds(0, own_blocks)], book_sem)
+    load.start()
+    asked[0] = want_ref[o]
+    own = pltpu.make_async_copy(want_ref.at[o], ids.at[0], smem_sem.at[0])
+    own.start()
+    pl.semaphore_wait(barrier, n_code - 1 + n_y - 1 + 1)
+
+    asks = []
+    for k in range(1, n_code):
+        peer = flip(o, k)
+        copy = remote(want_ref.at[peer], asked.at[k], id_send.at[k], id_recv.at[k], d, peer)
+        copy.start()
+        asks.append(copy)
+
+    def gate(kb, c):
+        count = counts_ref[kb]
+        for k in range(n_code):
+            slot = turn(k)
+            hit = jnp.float32(1e30)
+            for l in range(LIST_MAX):
+                same = (slots_ref[kb, l] == slot) & (count > l)
+                hit = jnp.where(same, jnp.float32(0.0), hit)
+            less[kb, k] = hit
+        return c
+
+    def serve_copy(k):
+        peer = flip(o, k)
+        return remote(served.at[k], fetched.at[k], f_send.at[k], f_recv.at[k], d, peer)
+
+    def move(k):
+        return pltpu.make_async_copy(asked.at[k], ids.at[k], smem_sem.at[k])
+
+    load.wait()
+    own.wait()
+    first = unnorm[n_code - 1, ids[0, 0, 0]]
+    served[0] = first
+    fetched[0] = first
+    serves = []
+    for k in range(1, n_code + 1):
+        if k < n_code:
+            asks[k - 1].wait_recv()
+            move(k).start()
+        if k > 1:
+            move(k - 1).wait()
+            served[k - 1] = unnorm[n_code - 1, ids[k - 1, 0, 0]]
+            copy = serve_copy(k - 1)
+            copy.start()
+            serves.append(copy)
+
+    kext[:, 128:256] = jnp.ones((keys, 128), jnp.bfloat16)
+    kext[:, 0:128] = keys_ref[...]
+
+    def turn_keys(c, carry):
+        at = pl.ds(pl.multiple_of(c * block, block), block)
+        turned = jnp.transpose(keys_ref[at, :])
+        kst[0:128, at] = turned
+        kst[128:256, at] = turned
+        return carry
+
+    lax.fori_loop(0, key_blocks, turn_keys, 0)
+    lax.fori_loop(0, key_blocks, gate, 0)
+
+    def score(k, blocks):
+        value = blocks[k]
         scaled = value * scale
         hi = scaled.astype(jnp.bfloat16)
-        words[s, :, 0:128] = hi
-        words[s, :, 128:256] = (scaled - hi.astype(jnp.float32)).astype(jnp.bfloat16)
+        words[:, 0:128] = hi
+        words[:, 128:256] = (scaled - hi.astype(jnp.float32)).astype(jnp.bfloat16)
         half = (0.5 * scale) * jnp.sum(value * value, axis=1, keepdims=True)
-        norms[s] = jnp.broadcast_to(half, (CBLK, 128))
-        return c
-
-    lax.fori_loop(0, n_code, prepare, 0)
-    kext[:, 0:128] = keys_ref[...]
-    kext[:, 128:256] = jnp.ones((key_blocks * block, 128), jnp.bfloat16)
-    post[key_blocks * LIST_MAX] = jnp.zeros((CBLK, block), jnp.bfloat16)
-
-    def key_block(kb, c):
-        keys = keys_ref[pl.ds(pl.multiple_of(kb * block, block), block), :]
-        turned = jnp.transpose(keys)
-        kst[0:128, :] = turned
-        kst[128:256, :] = turned
-        count = counts_ref[kb]
-        slots = [slots_ref[kb, l] for l in range(LIST_MAX)]
-        picked = jnp.concatenate([words[slots[l]] for l in range(LIST_MAX)], axis=0)
-        raw = jnp.dot(picked, kst[...], preferred_element_type=jnp.float32)
-        top = jnp.full((8, block), -3e38, jnp.float32)
-        for l in range(LIST_MAX):
-            rows = slice(l * CBLK, (l + 1) * CBLK)
-            less = norms[slots[l]] + jnp.where(l < count, 0.0, 1e30)
-            s = raw[rows] - jnp.tile(less, (1, block // 128))
-            scores[rows, :] = s
-            top = jnp.maximum(top, jnp.max(s.reshape(CBLK // 8, 8, block), axis=0))
-        peak = jnp.max(top, axis=0, keepdims=True)
-        total = jnp.zeros((8, block), jnp.float32)
-        for l in range(LIST_MAX):
-            rows = slice(l * CBLK, (l + 1) * CBLK)
-            e = jnp.exp2(scores[rows, :] - peak)
-            scores[rows, :] = e
-            total = total + jnp.sum(e.reshape(CBLK // 8, 8, block), axis=0)
-        total = jnp.sum(total, axis=0, keepdims=True)
-        logsum_ref[kb] = peak * math.log(2.0) + jnp.log(total)
-        inv = 1.0 / total
-        for l in range(LIST_MAX):
-            rows = slice(l * CBLK, (l + 1) * CBLK)
-            post[kb * LIST_MAX + l] = (scores[rows, :] * inv).astype(jnp.bfloat16)
-        return c
-
-    lax.fori_loop(0, key_blocks, key_block, 0)
-
-    def collect(slot):
-        for kb in range(key_blocks):
-            entry = key_blocks * LIST_MAX
-            for l in range(LIST_MAX):
-                hit = (slots_ref[kb, l] == slot) & (counts_ref[kb] > l)
-                entry = jnp.where(hit, kb * LIST_MAX + l, entry)
+        norms[...] = jnp.broadcast_to(half, (CBLK, 128))
+
+        def some(i, c):
+            for u in range(8):
+                q = i * 8 + u
+                cols = pl.ds(pl.multiple_of(q * 256, 256), 256)
+                right = kst[:, cols]
+                for h in range(2):
+                    rows = slice(h * 128, (h + 1) * 128)
+                    raw = jnp.dot(words[rows, :], right, preferred_element_type=jnp.float32)
+                    s = raw - jnp.tile(norms[rows, :], (1, 2))
+                    s = s.reshape(16, 8, 256)
+                    top = jnp.max(s, axis=0)
+                    e = jnp.exp2(s - top[None])
+                    peaks[k, h, :, cols] = top
+                    totals[k, h, :, cols] = jnp.sum(e, axis=0)
+                    e = e.reshape(128, 256)
+                    unnorm[k, 2 * q, rows, :] = e[:, 0:128]
+                    unnorm[k, 2 * q + 1, rows, :] = e[:, 128:256]
+            return c
+
+        lax.fori_loop(0, keys // 256 // 8, some, 0)
+
+    def normalise(last):
+        def one(kb, c):
+            cols = pl.ds(pl.multiple_of(kb * block, block), block)
+            top = jnp.full((8, block), -3e38, jnp.float32)
+            for k in range(n_code):
+                for h in range(2):
+                    top = jnp.maximum(top, peaks[k, h, :, cols] - less[kb, k])
+            peak = jnp.max(top, axis=0, keepdims=True)
+            total = jnp.zeros((8, block), jnp.float32)
+            for k in range(n_code):
+                for h in range(2):
+                    w = jnp.exp2((peaks[k, h, :, cols] - less[kb, k]) - peak)
+                    total = total + w * totals[k, h, :, cols]
+                    peaks[k, h, :, cols] = w
+            total = jnp.sum(total, axis=0, keepdims=True)
+            if last:
+                logsum_ref[kb] = peak * math.log(2.0) + jnp.log(total)
+            inv = 1.0 / total
+            for k in range(n_code):
+                for h in range(2):
+                    peaks[k, h, :, cols] = peaks[k, h, :, cols] * inv
+            return c
+
+        lax.fori_loop(0, key_blocks, one, 0)
+
+    def collect(k):
+        total = None
+        for q in range(keys // 512):
+            halves = []
+            for h in range(2):
+                rows = slice(h * 128, (h + 1) * 128)
+                tiles = []
+                for u in range(4):
+                    e = unnorm[k, q * 4 + u, rows, :].reshape(16, 8, 128)
+                    w = peaks[k, h, :, pl.ds((q * 4 + u) * 128, 128)]
+                    tiles.append((e * w[None]).reshape(128, 128).astype(jnp.bfloat16))
+                halves.append(jnp.concatenate(tiles, axis=1))
             piece = jnp.dot(
-                post[entry], kext[kb * block : (kb + 1) * block, :],
+                jnp.concatenate(halves, axis=0), kext[q * 512 : (q + 1) * 512, :],
                 preferred_element_type=jnp.float32,
             )
-            if kb == 0:
-                part[...] = piece
-            else:
-                part[...] += piece
+            total = piece if total is None else total + piece
+        part[...] = total
         for h in range(2):
             turned = jnp.transpose(part[h * 128 : (h + 1) * 128, 128:256])
-            sums[slot, CBLK + h : CBLK + h + 1, :] = turned[0:1, :]
-        sums[slot, CBLK + 2 :, :] = want_ref[slot, 2:, :].astype(jnp.float32)
-        sums[slot, :CBLK, :] = part[:, 0:128]
-
-    def turn(k):
-        out = o
-        bit = 1
-        while bit < n_code:
-            out = out + bit * (k // bit % 2) * (1 - 2 * (o // bit % 2))
-            bit *= 2
-        return out
-
-    def across(k):
-        peer = turn(k)
-        return remote(
-            sums.at[peer], con_ref.at[d * n_code + o], a_send.at[k], a_recv.at[k], d, peer
-        )
-
-    far = n_code // 2
-    collect(turn(far))
-    pl.semaphore_wait(barrier, n_code - 1 + n_y - 1 + 1)
-
-    def step(k, c):
-        collect(turn(k))
-        across(k - 1).start()
-        return c
-
-    lax.fori_loop(far + 1, n_code, step, 0)
-    collect(o)
-    across(n_code - 1).start()
-    own = pltpu.make_async_copy(sums.at[o], con_ref.at[d * n_code + o], own_sem)
-    own.start()
+            sums[k, CBLK + h : CBLK + h + 1, :] = turned[0:1, :]
+        sums[k, CBLK + 2 :, :] = want_ref[turn(k), 2:, :].astype(jnp.float32)
+        sums[k, :CBLK, :] = part[:, 0:128]
 
     def held(k, j):
         return ((y + n_y - j) % n_y * 2 + core) * n_code + flip(o, k)
 
-    sends = []
-
-    def to_y(k, j):
-        row = held(k, 0)
-        copy = remote(
-            con_ref.at[row], con_ref.at[row], y_send.at[j, k], y_recv.at[j, k],
-            (y + j) % n_y * 2 + core, o,
-        )
-        copy.start()
-        sends.append(copy)
-        return copy
-
-    def to_mate(k, j):
-        row = held(k, j)
-        copy = remote(
-            con_ref.at[row], con_ref.at[row], c_send.at[j, k], c_recv.at[j, k], mate, o
-        )
-        copy.start()
-        sends.append(copy)
-        return copy
-
-    if reply:
-        acc[...] = jnp.zeros_like(acc)
-
-    def absorb(row):
-        if not reply:
-            return
-        here = con_ref[row, pl.ds(CBLK + 2, 1), :]
-
-        def one(i, c):
-            same = (asked_ref[i, pl.ds(0, 1), :].astype(jnp.float32) == here).astype(jnp.float32)
-            acc[i] += con_ref[row] * same
+    order = list(range(1, n_code)) + [0]
+    backs = []
+    for sweep in range(sweeps):
+        reply = sweep + 1 < sweeps
+        con_ref = con_refs[sweep]
+        blocks = fetched if sweep == 0 else back
+
+        def scoring(k, c):
+            @pl.when(k > 0)
+            def _():
+                if sweep == 0:
+                    serve_copy_at(k).wait_recv()
+                else:
+                    back_copy_at(k).wait_recv()
+
+            score(k, blocks)
             return c
 
-        lax.fori_loop(0, n_code, one, 0)
-
-    y_copies = {}
-    mates = {}
-    own.wait()
-    for j in range(1, n_y):
-        y_copies[j, 0] = to_y(0, j)
-    mates[0, 0] = to_mate(0, 0)
-
-    def near(k, c):
-        collect(turn(k))
-
-        @pl.when(k > 1)
-        def _():
+        def serve_copy_at(k):
+            return remote(served.at[k], fetched.at[k], f_send.at[k], f_recv.at[k], d, turn(k))
+
+        def back_copy_at(k):
+            return remote(stage.at[k], back.at[k], b_send.at[k], b_recv.at[k], d, turn(k))
+
+        lax.fori_loop(0, n_code, scoring, 0)
+        normalise(not reply)
+
+        def across(k):
+            return remote(
+                sums.at[k], con_ref.at[d * n_code + o],
+                a_send.at[sweep, k], a_recv.at[sweep, k], d, turn(k),
+            )
+
+        collect(far)
+
+        def step(k, c):
+            collect(k)
             across(k - 1).start()
-
-        return c
-
-    lax.fori_loop(1, far, near, 0)
-    absorb(held(0, 0))
-    across(far - 1).start()
-
-    for k in range(1, n_code):
-        across(k).wait_recv()
-        for j in range(1, n_y):
-            y_copies[j, k] = to_y(k, j)
-        mates[0, k] = to_mate(k, 0)
-        absorb(held(k, 0))
-    for k in range(n_code):
-        for j in range(1, n_y):
-            y_copies[j, k].wait_recv()
-            mates[j, k] = to_mate(k, j)
-            absorb(held(k, j))
-        mates[0, k].wait_recv()
-        absorb(held(k, 0) + (1 - 2 * core) * n_code)
-    for k in range(n_code):
-        for j in range(1, n_y):
-            mates[j, k].wait_recv()
-            absorb(held(k, j) + (1 - 2 * core) * n_code)
-    if reply:
-        order = list(range(far, n_code)) + list(range(1, far))
-        for k in order + [0]:
-            peer = flip(o, k)
-            for h in range(2):
-                inv = 1.0 / (acc[peer, pl.ds(CBLK + h, 1), :] + 1.0)
-                column = jnp.transpose(jnp.broadcast_to(inv, (128, 128)))
-                rows = pl.ds(h * 128, 128)
-                fresh = (acc[peer, rows, :] + served_ref[peer, rows, :]) * column
-                if k == 0:
-                    back_ref[o, rows, :] = fresh
-                else:
-                    stage[k, rows, :] = fresh
-        backs = []
-        for k in order:
+            return c
+
+        lax.fori_loop(far + 1, n_code, step, 0)
+        collect(0)
+        across(n_code - 1).start()
+        mine = pltpu.make_async_copy(sums.at[0], con_ref.at[d * n_code + o], own_sem)
+        mine.start()
+
+        sends = []
+
+        def to_y(k, j):
+            row = held(k, 0)
             copy = remote(
-                stage.at[k], back_ref.at[o], b_send.at[k], b_recv.at[k], d, flip(o, k)
+                con_ref.at[row], con_ref.at[row],
+                y_send.at[sweep, j, k], y_recv.at[sweep, j, k],
+                (y + j) % n_y * 2 + core, o,
             )
             copy.start()
-            backs.append(copy)
-        for copy in backs:
-            copy.wait()
-    for k in range(1, n_code):
-        across(k).wait_send()
-    for copy in sends:
+            sends.append(copy)
+            return copy
+
+        def to_mate(k, j):
+            row = held(k, j)
+            copy = remote(
+                con_ref.at[row], con_ref.at[row],
+                c_send.at[sweep, j, k], c_recv.at[sweep, j, k], mate, o,
+            )
+            copy.start()
+            sends.append(copy)
+            return copy
+
+        if reply:
+            acc[...] = jnp.zeros_like(acc)
+
+        def absorb(row):
+            if not reply:
+                return
+            here = con_ref[row, pl.ds(CBLK + 2, 1), :]
+
+            def one(i, c):
+                same = (asked[i, pl.ds(0, 1), :].astype(jnp.float32) == here).astype(jnp.float32)
+                acc[i] += con_ref[row] * same
+                return c
+
+            lax.fori_loop(0, n_code, one, 0)
+
+        y_copies = {}
+        mates = {}
+        mine.wait()
+        for j in range(1, n_y):
+            y_copies[j, 0] = to_y(0, j)
+        mates[0, 0] = to_mate(0, 0)
+
+        def near(k, c):
+            collect(k)
+
+            @pl.when(k > 1)
+            def _():
+                across(k - 1).start()
+
+            return c
+
+        lax.fori_loop(1, far, near, 0)
+        absorb(held(0, 0))
+        across(far - 1).start()
+
+        for k in range(1, n_code):
+            across(k).wait_recv()
+            for j in range(1, n_y):
+                y_copies[j, k] = to_y(k, j)
+            mates[0, k] = to_mate(k, 0)
+            absorb(held(k, 0))
+        for k in range(n_code):
+            for j in range(1, n_y):
+                y_copies[j, k].wait_recv()
+                mates[j, k] = to_mate(k, j)
+                absorb(held(k, j))
+            mates[0, k].wait_recv()
+            absorb(held(k, 0) + (1 - 2 * core) * n_code)
+        for k in range(n_code):
+            for j in range(1, n_y):
+                mates[j, k].wait_recv()
+                absorb(held(k, j) + (1 - 2 * core) * n_code)
+        if reply:
+            for at, k in enumerate(order):
+                for h in range(2):
+                    inv = 1.0 / (acc[k, pl.ds(CBLK + h, 1), :] + 1.0)
+                    column = jnp.transpose(jnp.broadcast_to(inv, (128, 128)))
+                    rows = pl.ds(h * 128, 128)
+                    fresh = (acc[k, rows, :] + served[k, rows, :]) * column
+                    if k == 0:
+                        back[0, rows, :] = fresh
+                    else:
+                        stage[k, rows, :] = fresh
+                if at > 0:
+                    copy = back_copy_at(order[at - 1])
+                    copy.start()
+                    backs.append(copy)
+        for k in range(1, n_code):
+            across(k).wait_send()
+        for copy in sends:
+            copy.wait_send()
+    for copy in asks + serves + backs:
         copy.wait_send()
 
 
@@ -589,23 +685,6 @@
         return pltpu.CompilerParams(vmem_limit_bytes=VLIMIT, **kw)
 
     book = codebook.reshape(own_blocks, CBLK, feature)
-    fetched, served, asked = pl.pallas_call(
-        functools.partial(fetch_kernel, n_code),
-        out_shape=(blocks, blocks, jax.ShapeDtypeStruct((n_code, 8, 128), jnp.int32)),
-        in_specs=[VM, ANY],
-        out_specs=(VM, VM, VM),
-        scratch_shapes=[
-            pltpu.VMEM((own_blocks, CBLK, feature), f32),
-            pltpu.SMEM((n_code, 8, 128), jnp.int32),
-            dma((n_code,)), dma((n_code,)), dma((n_code,)), dma((n_code,)),
-            dma, dma, dma((n_code,)),
-        ],
-        compiler_params=params(collective_id=0, has_side_effects=True),
-    )(want, book)
-    logsum = None
-    gathered = []
-    current = book
-    joint = ITERS * n * (CBLK + MROWS) * feature * 4 <= HELD_BYTES
 
     def finish(parts, held):
         return pl.pallas_call(
@@ -623,6 +702,68 @@
             compiler_params=params(),
         )(*parts, held)
 
+    keys = key_blocks * block
+    joint = (
+        ITERS * n * (CBLK + MROWS) * feature * 4 <= HELD_BYTES
+        and own_blocks * 128 <= keys
+        and n_code * CBLK * keys * 4 <= HELD_BYTES * 2 + HELD_BYTES // 2
+        and keys % 2048 == 0 and block % 512 == 0
+    )
+    if joint:
+        bf16 = jnp.bfloat16
+        results = pl.pallas_call(
+            functools.partial(
+                sweeps_kernel, n_dp, n_code, key_blocks, block, own_blocks, feature, ITERS
+            ),
+            out_shape=(con_shape,) * ITERS
+            + (jax.ShapeDtypeStruct((key_blocks, 1, block), f32),),
+            in_specs=[SM, SM, VM, VM, ANY],
+            out_specs=(VM,) * (ITERS + 1),
+            scratch_shapes=[
+                pltpu.VMEM((n_code, keys // 128, CBLK, 128), f32),
+                pltpu.VMEM((n_code, 2, 8, keys), f32),
+                pltpu.VMEM((n_code, 2, 8, keys), f32),
+                pltpu.VMEM((CBLK, 256), bf16),
+                pltpu.VMEM((CBLK, 128), f32),
+                pltpu.VMEM((256, keys), bf16),
+                pltpu.VMEM((keys, 256), bf16),
+                pltpu.VMEM(sums_shape.shape, f32),
+                pltpu.VMEM(sums_shape.shape, f32),
+                pltpu.VMEM(blocks.shape, f32),
+                pltpu.VMEM(blocks.shape, f32),
+                pltpu.VMEM(blocks.shape, f32),
+                pltpu.VMEM(blocks.shape, f32),
+                pltpu.VMEM((n_code, 8, 128), jnp.int32),
+                pltpu.VMEM((CBLK, 256), f32),
+                pltpu.SMEM((key_blocks, n_code), f32),
+                pltpu.SMEM((n_code, 8, 128), jnp.int32),
+                dma((n_code,)), dma((n_code,)),
+                dma((n_code,)), dma((n_code,)),
+                dma((n_code,)), dma((n_code,)),
+                dma((ITERS, n_code)), dma((ITERS, n_code)),
+                dma((ITERS, n_y, n_code)), dma((ITERS, n_y, n_code)),
+                dma((ITERS, n_y, n_code)), dma((ITERS, n_y, n_code)),
+                dma, dma, dma((n_code,)),
+            ],
+            compiler_params=params(collective_id=0, has_side_effects=True),
+        )(slots, counts, want, cached_keys, book)
+        current = finish(results[:ITERS], book)
+        return (current.reshape(own_rows, feature), results[ITERS].reshape(-1))
+
+    fetched, served, asked = pl.pallas_call(
+        functools.partial(fetch_kernel, n_code),
+        out_shape=(blocks, blocks, jax.ShapeDtypeStruct((n_code, 8, 128), jnp.int32)),
+        in_specs=[VM, ANY],
+        out_specs=(VM, VM, VM),
+        scratch_shapes=[
+            pltpu.VMEM((own_blocks, CBLK, feature), f32),
+            pltpu.SMEM((n_code, 8, 128), jnp.int32),
+            dma((n_code,)), dma((n_code,)), dma((n_code,)), dma((n_code,)),
+            dma, dma, dma((n_code,)),
+        ],
+        compiler_params=params(collective_id=0, has_side_effects=True),
+    )(want, book)
+    current = book
     for sweep in range(ITERS):
         reply = sweep + 1 < ITERS
         sems = [
@@ -631,86 +772,46 @@
             dma((n_y, n_code)), dma((n_y, n_code)),
             dma,
         ]
-        if joint:
-            ins = [slots, counts, fetched, cached_keys, want]
-            outs = [con_shape, jax.ShapeDtypeStruct((key_blocks, 1, block), f32)]
-            scratch = []
-            if reply:
-                ins += [served, asked]
-                outs += [blocks]
-                scratch = [
-                    pltpu.VMEM(sums_shape.shape, f32), pltpu.VMEM(blocks.shape, f32),
-                    dma((n_code,)), dma((n_code,)),
-                ]
-            scratch += [
+        sums, logsum = pl.pallas_call(
+            functools.partial(assign_kernel, n_code, key_blocks, block, feature),
+            out_shape=(sums_shape, jax.ShapeDtypeStruct((key_blocks, 1, block), f32)),
+            in_specs=[SM, SM, VM, VM, VM],
+            out_specs=(VM, VM),
+            scratch_shapes=[
                 pltpu.VMEM((n_code, CBLK, 256), jnp.bfloat16),
                 pltpu.VMEM((n_code, CBLK, 128), f32),
                 pltpu.VMEM((256, block), jnp.bfloat16),
-                pltpu.VMEM((key_blocks * block, 256), jnp.bfloat16),
+                pltpu.VMEM((block, 256), jnp.bfloat16),
+                pltpu.VMEM((LIST_MAX * CBLK, 256), jnp.bfloat16),
                 pltpu.VMEM((LIST_MAX * CBLK, block), f32),
-                pltpu.VMEM((key_blocks * LIST_MAX + 1, CBLK, block), jnp.bfloat16),
-                pltpu.VMEM(sums_shape.shape, f32),
-                pltpu.VMEM((CBLK, 256), f32),
-            ] + sems
-            results = pl.pallas_call(
-                functools.partial(
-                    fused_kernel, n_dp, n_code, key_blocks, block, feature, reply
-                ),
-                out_shape=tuple(outs),
-                in_specs=[SM, SM] + [VM] * (len(ins) - 2),
-                out_specs=(VM,) * len(outs),
-                scratch_shapes=scratch,
-                compiler_params=params(collective_id=1 + sweep, has_side_effects=True),
-            )(*ins)
-            con, logsum = results[:2]
-            if reply:
-                fetched = results[2]
-        else:
-            sums, logsum = pl.pallas_call(
-                functools.partial(assign_kernel, n_code, key_blocks, block, feature),
-                out_shape=(sums_shape, jax.ShapeDtypeStruct((key_blocks, 1, block), f32)),
-                in_specs=[SM, SM, VM, VM, VM],
+                pltpu.VMEM((LIST_MAX * CBLK, block), jnp.bfloat16),
+                pltpu.VMEM((n_code, CBLK, 256), f32),
+            ],
+            compiler_params=params(),
+        )(slots, counts, fetched, cached_keys, want)
+        if reply:
+            con, fetched = pl.pallas_call(
+                functools.partial(exchange_kernel, n_dp, n_code, True),
+                out_shape=(con_shape, blocks),
+                in_specs=[VM, VM, VM],
                 out_specs=(VM, VM),
                 scratch_shapes=[
-                    pltpu.VMEM((n_code, CBLK, 256), jnp.bfloat16),
-                    pltpu.VMEM((n_code, CBLK, 128), f32),
-                    pltpu.VMEM((256, block), jnp.bfloat16),
-                    pltpu.VMEM((block, 256), jnp.bfloat16),
-                    pltpu.VMEM((LIST_MAX * CBLK, 256), jnp.bfloat16),
-                    pltpu.VMEM((LIST_MAX * CBLK, block), f32),
-                    pltpu.VMEM((LIST_MAX * CBLK, block), jnp.bfloat16),
-                    pltpu.VMEM((n_code, CBLK, 256), f32),
-                ],
-                compiler_params=params(),
-            )(slots, counts, fetched, cached_keys, want)
-            if reply:
-                con, fetched = pl.pallas_call(
-                    functools.partial(exchange_kernel, n_dp, n_code, True),
-                    out_shape=(con_shape, blocks),
-                    in_specs=[VM, VM, VM],
-                    out_specs=(VM, VM),
-                    scratch_shapes=[
-                        pltpu.VMEM(sums_shape.shape, f32), pltpu.VMEM(blocks.shape, f32)
-                    ] + sems + [dma((n_code,)), dma((n_code,))],
-                    compiler_params=params(collective_id=1 + sweep, has_side_effects=True),
-                )(sums, served, asked)
-            else:
-                con = pl.pallas_call(
-                    functools.partial(exchange_kernel, n_dp, n_code, False),
-                    out_shape=con_shape,
-                    in_specs=[VM],
-                    out_specs=VM,
-                    scratch_shapes=sems,
-                    compiler_params=params(collective_id=1 + sweep, has_side_effects=True),
-                )(sums)
-        gathered.append(con)
-        if not joint:
-            current = finish(gathered, current)
-            gathered = []
-            if reply:
-                current, fetched = lax.optimization_barrier((current, fetched))
-    if gathered:
-        current = finish(gathered, current)
+                    pltpu.VMEM(sums_shape.shape, f32), pltpu.VMEM(blocks.shape, f32)
+                ] + sems + [dma((n_code,)), dma((n_code,))],
+                compiler_params=params(collective_id=1 + sweep, has_side_effects=True),
+            )(sums, served, asked)
+        else:
+            con = pl.pallas_call(
+                functools.partial(exchange_kernel, n_dp, n_code, False),
+                out_shape=con_shape,
+                in_specs=[VM],
+                out_specs=VM,
+                scratch_shapes=sems,
+                compiler_params=params(collective_id=1 + sweep, has_side_effects=True),
+            )(sums)
+        current = finish([con], current)
+        if reply:
+            current, fetched = lax.optimization_barrier((current, fetched))
     return (current.reshape(own_rows, feature), logsum.reshape(-1))
 
 

time: 182 us -> 161 us (0.88)
  Pallas kernels: 178 us -> 157 us
    pallas_call x3 -> x1, Pallas kernels: 169 us -> 148 us  [on_device(): pl.pallas_call(functools.partial(sweeps_kernel, n_dp, n_code, key_blocks,...]
where the time goes in v1:
time: 161 us; the launch traced here: 160 us
  Pallas kernels  157 us (98%)
    pallas_call x1, Pallas kernels, on_device(): pl.pallas_call(functools.partial(sweeps_kernel, n_dp, n_code, key_blocks,...  148 us
    pallas_call x1, Pallas kernels, finish(): pl.pallas_call(functools.partial(finish_kernel, n, own_blocks, len(parts)...  8.88 us

profile of v1, /device:TPU:1, one launch (start us, length us, event | category | flops | bytes accessed | tf_op | source)
XLA Modules:
  0.0 160.0 jit_solution(8513122108628506360)
XLA Ops:
  0.6 0.7 add_select_fusion
  1.3 0.0 copy-start
  1.3 0.1 broadcast_in_dim.21
  1.4 0.1 eq.17
  1.5 0.1 select_reduce_fusion
  1.6 0.7 broadcast_in_dim.24.refs_2_
  2.3 0.0 copy-done
  2.3 148.2 %shard_map.59 = (f32[32,264,128]{2,1,0:T(8,128)}, f32[32,264,128]{2,1,0:T(8,128)}, f32[8,1,512]{2,1,0:T(1,128)}) custom-call(s32[8,6]{1,0:T(8,128)} %copy-done, s32[8]{0:T(128)} %refs_1_.1, s32[8,8,128]{2,1,0:T(8,128)} %broadcast_in_dim.24.refs_2_, bf16[4096,128]{1,0:T(8,128)(2,1)} %refs_3_.1, f32[32,256,128]{2,1,0:T(8,128)} %bitcast.4), custom_call_target="tpu_custom_call" | custom-call | tf_op jit(solution)/shard_map/pallas_call | solution.py:714
  150.5 0.0 copy-start.1
  150.5 8.9 %shard_map.60 = f32[32,256,128]{2,1,0:T(8,128)} custom-call(f32[32,264,128]{2,1,0:T(8,128)} %get-tuple-element.5.refs_0_, f32[32,264,128]{2,1,0:T(8,128)} %get-tuple-element.6.refs_1_, f32[32,256,128]{2,1,0:T(8,128)} %bitcast.5), custom_call_target="tpu_custom_call" | custom-call | tf_op jit(solution)/shard_map/pallas_call | solution.py:690
  159.4 0.0 copy-done.1
  159.4 0.6 copy.7
Async XLA Ops:
  1.3 1.0 copy-start
  150.5 8.9 %copy-start.1 = (f32[8,1,512]{2,1,0:T(1,128)S(1)}, f32[8,1,512]{2,1,0:T(1,128)}, u32[]{:S(2)}) copy-start(f32[8,1,512]{2,1,0:T(1,128)} %get-tuple-element.7) | copy-start | bytes 49156

commit v2 on v1

--- a/solution.py
+++ b/solution.py
@@ -390,10 +390,37 @@
         sums[k, :CBLK, :] = part[:, 0:128]
 
     def held(k, j):
-        return ((y + n_y - j) % n_y * 2 + core) * n_code + flip(o, k)
+        return ((y + n_y - j) % n_y * 2 + core) * n_code + turn(k)
 
     order = list(range(1, n_code)) + [0]
     backs = []
+    wide = list(range(far, n_code))
+    close = list(range(2, far))
+    beside = list(range(1, min(2, far)))
+    beside = list(range(1, min(2, far)))
+    inner = wide[:1] + close + wide[1:2] + [0] + beside + wide[2:]
+    outer = close + [0] + wide[:1] + beside + wide[1:]
+    inner_in = close + wide[:2] + beside + wide[2:]
+    outer_in = beside + wide[:1] + wide[2:] + close[:1] + wide[1:2] + close[1:]
+    middle = (o // far % 2) != (o // max(far // 2, 1) % 2)
+
+    def choose(i, first, second):
+        return jnp.where(middle, first[i], second[i])
+
+    def pick(p):
+        out = choose(0, inner, outer)
+        for i in range(1, n_code):
+            out = jnp.where(p == i, choose(i, inner, outer), out)
+        return out
+
+    waits = [("y", i) for i in range(n_code)]
+    events = [("a", i) for i in range(min(far, n_code - 1))]
+    for i in range(len(events), n_code - 1):
+        take = 2 if i < n_code - 2 else 1
+        events += waits[:take] + [("a", i)]
+        waits = waits[take:]
+    events += waits
+
     for sweep in range(sweeps):
         reply = sweep + 1 < sweeps
         con_ref = con_refs[sweep]
@@ -425,41 +452,33 @@
                 a_send.at[sweep, k], a_recv.at[sweep, k], d, turn(k),
             )
 
-        collect(far)
-
-        def step(k, c):
-            collect(k)
-            across(k - 1).start()
-            return c
-
-        lax.fori_loop(far + 1, n_code, step, 0)
-        collect(0)
-        across(n_code - 1).start()
-        mine = pltpu.make_async_copy(sums.at[0], con_ref.at[d * n_code + o], own_sem)
-        mine.start()
-
-        sends = []
-
         def to_y(k, j):
             row = held(k, 0)
-            copy = remote(
+            return remote(
                 con_ref.at[row], con_ref.at[row],
                 y_send.at[sweep, j, k], y_recv.at[sweep, j, k],
                 (y + j) % n_y * 2 + core, o,
             )
-            copy.start()
-            sends.append(copy)
-            return copy
+
+        def own_y(j):
+            return remote(
+                sums.at[0], con_ref.at[d * n_code + o],
+                y_send.at[sweep, j, 0], y_recv.at[sweep, j, 0],
+                (y + j) % n_y * 2 + core, o,
+            )
+
+        def own_mate():
+            return remote(
+                sums.at[0], con_ref.at[d * n_code + o],
+                c_send.at[sweep, 0, 0], c_recv.at[sweep, 0, 0], mate, o,
+            )
 
         def to_mate(k, j):
             row = held(k, j)
-            copy = remote(
+            return remote(
                 con_ref.at[row], con_ref.at[row],
                 c_send.at[sweep, j, k], c_recv.at[sweep, j, k], mate, o,
             )
-            copy.start()
-            sends.append(copy)
-            return copy
 
         if reply:
             acc[...] = jnp.zeros_like(acc)
@@ -476,43 +495,61 @@
 
             lax.fori_loop(0, n_code, one, 0)
 
-        y_copies = {}
-        mates = {}
+        mine = pltpu.make_async_copy(sums.at[0], con_ref.at[d * n_code + o], own_sem)
+
+        def depart(k):
+            @pl.when(k > 0)
+            def _():
+                across(k).start()
+
+            @pl.when(k == 0)
+            def _():
+                mine.start()
+                for j in range(1, n_y):
+                    own_y(j).start()
+                own_mate().start()
+
+        def produce(p, c):
+            collect(pick(p))
+
+            @pl.when(p > 0)
+            def _():
+                depart(pick(p - 1))
+
+            return c
+
+        lax.fori_loop(0, n_code, produce, 0)
         mine.wait()
-        for j in range(1, n_y):
-            y_copies[j, 0] = to_y(0, j)
-        mates[0, 0] = to_mate(0, 0)
-
-        def near(k, c):
-            collect(k)
-
-            @pl.when(k > 1)
-            def _():
-                across(k - 1).start()
-
-            return c
-
-        lax.fori_loop(1, far, near, 0)
+        depart(pick(n_code - 1))
         absorb(held(0, 0))
-        across(far - 1).start()
-
+        for kind, i in events:
+            if kind == "a":
+                k = choose(i, inner_in, outer_in)
+                across(k).wait_recv()
+                for j in range(1, n_y):
+                    to_y(k, j).start()
+                to_mate(k, 0).start()
+                absorb(held(k, 0))
+            else:
+                k = choose(i - 1, inner_in, outer_in) if i else 0
+                for j in range(1, n_y):
+                    to_y(k, j).wait_recv()
+                    to_mate(k, j).start()
+                    absorb(held(k, j))
+                to_mate(k, 0).wait_recv()
+                absorb(held(k, 0) + (1 - 2 * core) * n_code)
+        for i in range(n_code):
+            k = choose(i - 1, inner_in, outer_in) if i else 0
+            for j in range(1, n_y):
+                to_mate(k, j).wait_recv()
+                absorb(held(k, j) + (1 - 2 * core) * n_code)
         for k in range(1, n_code):
-            across(k).wait_recv()
-            for j in range(1, n_y):
-                y_copies[j, k] = to_y(k, j)
-            mates[0, k] = to_mate(k, 0)
-            absorb(held(k, 0))
+            across(k).wait_send()
         for k in range(n_code):
             for j in range(1, n_y):
-                y_copies[j, k].wait_recv()
-                mates[j, k] = to_mate(k, j)
-                absorb(held(k, j))
-            mates[0, k].wait_recv()
-            absorb(held(k, 0) + (1 - 2 * core) * n_code)
-        for k in range(n_code):
-            for j in range(1, n_y):
-                mates[j, k].wait_recv()
-                absorb(held(k, j) + (1 - 2 * core) * n_code)
+                to_y(k, j).wait_send()
+                to_mate(k, j).wait_send()
+            to_mate(k, 0).wait_send()
         if reply:
             for at, k in enumerate(order):
                 for h in range(2):
@@ -528,10 +565,6 @@
                     copy = back_copy_at(order[at - 1])
                     copy.start()
                     backs.append(copy)
-        for k in range(1, n_code):
-            across(k).wait_send()
-        for copy in sends:
-            copy.wait_send()
     for copy in asks + serves + backs:
         copy.wait_send()
 

time: 161 us -> 147 us (0.913)
  Pallas kernels: 157 us -> 143 us
    pallas_call x1, Pallas kernels: 148 us -> 134 us  [on_device(): pl.pallas_call(functools.partial(sweeps_kernel, n_dp, n_code, key_blocks,...]
where the time goes in v2:
time: 147 us; the launch traced here: 146 us
  Pallas kernels  143 us (97%)
  local copies, waits for them, and re-layouts  1.47 us (1%)
    pallas_call x1, Pallas kernels, on_device(): pl.pallas_call(functools.partial(sweeps_kernel, n_dp, n_code, key_blocks,...  134 us
    pallas_call x1, Pallas kernels, finish(): pl.pallas_call(functools.partial(finish_kernel, n, own_blocks, len(parts)...  8.88 us

profile of v2, /device:TPU:1, one launch (start us, length us, event | category | flops | bytes accessed | tf_op | source)
XLA Modules:
  0.0 145.9 jit_solution(11419507906931171089)
XLA Ops:
  0.6 0.7 add_select_fusion
  1.3 0.0 copy-start
  1.3 0.1 broadcast_in_dim.21
  1.4 0.1 eq.17
  1.5 0.1 select_reduce_fusion
  1.6 0.7 broadcast_in_dim.24.refs_2_
  2.3 0.0 copy-done
  2.3 134.1 %shard_map.59 = (f32[32,264,128]{2,1,0:T(8,128)}, f32[32,264,128]{2,1,0:T(8,128)}, f32[8,1,512]{2,1,0:T(1,128)}) custom-call(s32[8,6]{1,0:T(8,128)} %copy-done, s32[8]{0:T(128)} %refs_1_.1, s32[8,8,128]{2,1,0:T(8,128)} %broadcast_in_dim.24.refs_2_, bf16[4096,128]{1,0:T(8,128)(2,1)} %refs_3_.1, f32[32,256,128]{2,1,0:T(8,128)} %bitcast.4), custom_call_target="tpu_custom_call" | custom-call | tf_op jit(solution)/shard_map/pallas_call | solution.py:747
  136.4 0.0 copy-start.1
  136.4 8.9 %shard_map.60 = f32[32,256,128]{2,1,0:T(8,128)} custom-call(f32[32,264,128]{2,1,0:T(8,128)} %get-tuple-element.5.refs_0_, f32[32,264,128]{2,1,0:T(8,128)} %get-tuple-element.6.refs_1_, f32[32,256,128]{2,1,0:T(8,128)} %bitcast.5), custom_call_target="tpu_custom_call" | custom-call | tf_op jit(solution)/shard_map/pallas_call | solution.py:723
  145.2 0.0 copy-done.1
  145.3 0.6 copy.7
Async XLA Ops:
  1.3 1.0 copy-start
  136.4 8.9 %copy-start.1 = (f32[8,1,512]{2,1,0:T(1,128)S(1)}, f32[8,1,512]{2,1,0:T(1,128)}, u32[]{:S(2)}) copy-start(f32[8,1,512]{2,1,0:T(1,128)} %get-tuple-element.7) | copy-start | bytes 49156

commit v3 on v2

--- a/solution.py
+++ b/solution.py
@@ -212,13 +212,14 @@
 
 def sweeps_kernel(n_dp, n_code, key_blocks, block, own_blocks, feature, sweeps, *refs):
     slots_ref, counts_ref, want_ref, keys_ref, book_hbm = refs[:5]
-    con_refs = refs[5 : 5 + sweeps]
+    out_refs = refs[5 : 5 + sweeps]
     logsum_ref = refs[5 + sweeps]
-    (unnorm, peaks, totals, words, norms, kst, kext, sums, acc, stage, served,
+    con_refs = refs[6 + sweeps : 6 + 2 * sweeps]
+    (unnorm, peaks, run_top, run_total, words, norms, kst, kext, sums, acc, stage, served,
      fetched, back, asked, part, less, ids,
      id_send, id_recv, f_send, f_recv, b_send, b_recv,
      a_send, a_recv, y_send, y_recv, c_send, c_recv,
-     book_sem, own_sem, smem_sem) = refs[6 + sweeps :]
+     book_sem, own_sem, smem_sem, out_sem, keep_sem) = refs[6 + 2 * sweeps :]
     scale = math.log2(math.e) / math.sqrt(feature)
     keys = key_blocks * block
     chunks = keys // 128
@@ -324,6 +325,8 @@
                 q = i * 8 + u
                 cols = pl.ds(pl.multiple_of(q * 256, 256), 256)
                 right = kst[:, cols]
+                away = less[q * 256 // block, k]
+                tops, parts = [], []
                 for h in range(2):
                     rows = slice(h * 128, (h + 1) * 128)
                     raw = jnp.dot(words[rows, :], right, preferred_element_type=jnp.float32)
@@ -332,10 +335,17 @@
                     top = jnp.max(s, axis=0)
                     e = jnp.exp2(s - top[None])
                     peaks[k, h, :, cols] = top
-                    totals[k, h, :, cols] = jnp.sum(e, axis=0)
+                    tops.append(top - away)
+                    parts.append(jnp.sum(e, axis=0))
                     e = e.reshape(128, 256)
                     unnorm[k, 2 * q, rows, :] = e[:, 0:128]
                     unnorm[k, 2 * q + 1, rows, :] = e[:, 128:256]
+                old = run_top[:, cols]
+                new = jnp.maximum(old, jnp.maximum(tops[0], tops[1]))
+                run_top[:, cols] = new
+                run_total[:, cols] = run_total[:, cols] * jnp.exp2(old - new) + (
+                    parts[0] * jnp.exp2(tops[0] - new) + parts[1] * jnp.exp2(tops[1] - new)
+                )
             return c
 
         lax.fori_loop(0, keys // 256 // 8, some, 0)
@@ -343,24 +353,16 @@
     def normalise(last):
         def one(kb, c):
             cols = pl.ds(pl.multiple_of(kb * block, block), block)
-            top = jnp.full((8, block), -3e38, jnp.float32)
-            for k in range(n_code):
-                for h in range(2):
-                    top = jnp.maximum(top, peaks[k, h, :, cols] - less[kb, k])
+            top = run_top[:, cols]
             peak = jnp.max(top, axis=0, keepdims=True)
-            total = jnp.zeros((8, block), jnp.float32)
-            for k in range(n_code):
-                for h in range(2):
-                    w = jnp.exp2((peaks[k, h, :, cols] - less[kb, k]) - peak)
-                    total = total + w * totals[k, h, :, cols]
-                    peaks[k, h, :, cols] = w
-            total = jnp.sum(total, axis=0, keepdims=True)
+            total = jnp.sum(run_total[:, cols] * jnp.exp2(top - peak), axis=0, keepdims=True)
             if last:
-                logsum_ref[kb] = peak * math.log(2.0) + jnp.log(total)
-            inv = 1.0 / total
-            for k in range(n_code):
-                for h in range(2):
-                    peaks[k, h, :, cols] = peaks[k, h, :, cols] * inv
+                row = peak * math.log(2.0) + jnp.log(total)
+                for i in range(block // 128):
+                    at = pl.ds(kb * (block // 128) + i, 1)
+                    logsum_ref[at, :] = row[:, i * 128 : (i + 1) * 128]
+            run_top[:, cols] = jnp.broadcast_to(peak, (8, block))
+            run_total[:, cols] = jnp.broadcast_to(1.0 / total, (8, block))
             return c
 
         lax.fori_loop(0, key_blocks, one, 0)
@@ -374,7 +376,9 @@
                 tiles = []
                 for u in range(4):
                     e = unnorm[k, q * 4 + u, rows, :].reshape(16, 8, 128)
-                    w = peaks[k, h, :, pl.ds((q * 4 + u) * 128, 128)]
+                    cols = pl.ds((q * 4 + u) * 128, 128)
+                    w = (peaks[k, h, :, cols] - less[q * 512 // block, k]) - run_top[:, cols]
+                    w = jnp.exp2(w) * run_total[:, cols]
                     tiles.append((e * w[None]).reshape(128, 128).astype(jnp.bfloat16))
                 halves.append(jnp.concatenate(tiles, axis=1))
             piece = jnp.dot(
@@ -392,8 +396,7 @@
     def held(k, j):
         return ((y + n_y - j) % n_y * 2 + core) * n_code + turn(k)
 
-    order = list(range(1, n_code)) + [0]
-    backs = []
+    keeps = []
     wide = list(range(far, n_code))
     close = list(range(2, far))
     beside = list(range(1, min(2, far)))
@@ -407,11 +410,14 @@
     def choose(i, first, second):
         return jnp.where(middle, first[i], second[i])
 
+    def table(p, first, second):
+        out = choose(0, first, second)
+        for i in range(1, n_code):
+            out = jnp.where(p == i, choose(i, first, second), out)
+        return out
+
     def pick(p):
-        out = choose(0, inner, outer)
-        for i in range(1, n_code):
-            out = jnp.where(p == i, choose(i, inner, outer), out)
-        return out
+        return table(p, inner, outer)
 
     waits = [("y", i) for i in range(n_code)]
     events = [("a", i) for i in range(min(far, n_code - 1))]
@@ -421,10 +427,19 @@
         waits = waits[take:]
     events += waits
 
+    def serve_copy_at(k):
+        return remote(served.at[k], fetched.at[k], f_send.at[k], f_recv.at[k], d, turn(k))
+
+    def back_copy_at(k):
+        return remote(stage.at[k], back.at[k], b_send.at[k], b_recv.at[k], d, turn(k))
+
     for sweep in range(sweeps):
         reply = sweep + 1 < sweeps
         con_ref = con_refs[sweep]
         blocks = fetched if sweep == 0 else back
+
+        run_top[...] = jnp.full((8, keys), -3e38, jnp.float32)
+        run_total[...] = jnp.zeros((8, keys), jnp.float32)
 
         def scoring(k, c):
             @pl.when(k > 0)
@@ -437,12 +452,6 @@
             score(k, blocks)
             return c
 
-        def serve_copy_at(k):
-            return remote(served.at[k], fetched.at[k], f_send.at[k], f_recv.at[k], d, turn(k))
-
-        def back_copy_at(k):
-            return remote(stage.at[k], back.at[k], b_send.at[k], b_recv.at[k], d, turn(k))
-
         lax.fori_loop(0, n_code, scoring, 0)
         normalise(not reply)
 
@@ -485,6 +494,9 @@
 
         def absorb(row):
             if not reply:
+                pltpu.make_async_copy(
+                    con_ref.at[row], out_refs[sweep].at[row], out_sem.at[row]
+                ).start()
                 return
             here = con_ref[row, pl.ds(CBLK + 2, 1), :]
 
@@ -551,7 +563,8 @@
                 to_mate(k, j).wait_send()
             to_mate(k, 0).wait_send()
         if reply:
-            for at, k in enumerate(order):
+            for p in range(n_code):
+                k = (p + 1) % n_code
                 for h in range(2):
                     inv = 1.0 / (acc[k, pl.ds(CBLK + h, 1), :] + 1.0)
                     column = jnp.transpose(jnp.broadcast_to(inv, (128, 128)))
@@ -561,11 +574,20 @@
                         back[0, rows, :] = fresh
                     else:
                         stage[k, rows, :] = fresh
-                if at > 0:
-                    copy = back_copy_at(order[at - 1])
-                    copy.start()
-                    backs.append(copy)
-    for copy in asks + serves + backs:
+                if p > 0:
+                    back_copy_at(p).start()
+            keep = pltpu.make_async_copy(con_ref, out_refs[sweep], keep_sem.at[sweep])
+            keep.start()
+            keeps.append(keep)
+    for row in range(n_dp * n_code):
+        pltpu.make_async_copy(
+            con_refs[-1].at[row], out_refs[-1].at[row], out_sem.at[row]
+        ).wait()
+    for k in range(1, n_code):
+        back_copy_at(k).wait_send()
+    for keep in keeps:
+        keep.wait()
+    for copy in asks + serves:
         copy.wait_send()
 
 
@@ -749,13 +771,14 @@
                 sweeps_kernel, n_dp, n_code, key_blocks, block, own_blocks, feature, ITERS
             ),
             out_shape=(con_shape,) * ITERS
-            + (jax.ShapeDtypeStruct((key_blocks, 1, block), f32),),
+            + (jax.ShapeDtypeStruct((keys // 128, 128), f32),),
             in_specs=[SM, SM, VM, VM, ANY],
-            out_specs=(VM,) * (ITERS + 1),
-            scratch_shapes=[
+            out_specs=(ANY,) * ITERS + (VM,),
+            scratch_shapes=[pltpu.VMEM(con_shape.shape, f32) for _ in range(ITERS)] + [
                 pltpu.VMEM((n_code, keys // 128, CBLK, 128), f32),
                 pltpu.VMEM((n_code, 2, 8, keys), f32),
-                pltpu.VMEM((n_code, 2, 8, keys), f32),
+                pltpu.VMEM((8, keys), f32),
+                pltpu.VMEM((8, keys), f32),
                 pltpu.VMEM((CBLK, 256), bf16),
                 pltpu.VMEM((CBLK, 128), f32),
                 pltpu.VMEM((256, keys), bf16),
@@ -776,7 +799,7 @@
                 dma((ITERS, n_code)), dma((ITERS, n_code)),
                 dma((ITERS, n_y, n_code)), dma((ITERS, n_y, n_code)),
                 dma((ITERS, n_y, n_code)), dma((ITERS, n_y, n_code)),
-                dma, dma, dma((n_code,)),
+                dma, dma, dma((n_code,)), dma((n,)), dma((ITERS,)),
             ],
             compiler_params=params(collective_id=0, has_side_effects=True),
         )(slots, counts, want, cached_keys, book)

time: 147 us -> 143 us (0.973)
  Pallas kernels: 143 us -> 140 us
    pallas_call x1, Pallas kernels: 134 us -> 131 us  [on_device(): pl.pallas_call(functools.partial(sweeps_kernel, n_dp, n_code, key_blocks,...]
where the time goes in v3:
time: 143 us
  Pallas kernels  140 us (98%)
  local copies, waits for them, and re-layouts  1.47 us (1%)
    pallas_call x1, Pallas kernels, on_device(): pl.pallas_call(functools.partial(sweeps_kernel, n_dp, n_code, key_blocks,...  131 us
    pallas_call x1, Pallas kernels, finish(): pl.pallas_call(functools.partial(finish_kernel, n, own_blocks, len(parts)...  8.88 us

profile of v3, /device:TPU:1, one launch (start us, length us, event | category | flops | bytes accessed | tf_op | source)
XLA Modules:
  0.0 143.0 jit_solution(9218233293368214611)
XLA Ops:
  0.6 0.7 add_select_fusion
  1.3 0.0 copy-start
  1.3 0.1 broadcast_in_dim.21
  1.4 0.1 eq.17
  1.5 0.1 select_reduce_fusion
  1.6 0.7 broadcast_in_dim.24.refs_2_
  2.3 0.0 copy-done
  2.3 131.2 %shard_map.59 = (f32[32,264,128]{2,1,0:T(8,128)}, f32[32,264,128]{2,1,0:T(8,128)}, f32[32,128]{1,0:T(8,128)}) custom-call(s32[8,6]{1,0:T(8,128)} %copy-done, s32[8]{0:T(128)} %refs_1_.1, s32[8,8,128]{2,1,0:T(8,128)} %broadcast_in_dim.24.refs_2_, bf16[4096,128]{1,0:T(8,128)(2,1)} %refs_3_.1, f32[32,256,128]{2,1,0:T(8,128)} %bitcast.4), custom_call_target="tpu_custom_call" | custom-call | tf_op jit(solution)/shard_map/pallas_call | solution.py:769
  133.5 0.0 copy-start.1
  133.5 8.9 %shard_map.60 = f32[32,256,128]{2,1,0:T(8,128)} custom-call(f32[32,264,128]{2,1,0:T(8,128)} %get-tuple-element.5.refs_0_, f32[32,264,128]{2,1,0:T(8,128)} %get-tuple-element.6.refs_1_, f32[32,256,128]{2,1,0:T(8,128)} %bitcast.5), custom_call_target="tpu_custom_call" | custom-call | tf_op jit(solution)/shard_map/pallas_call | solution.py:745
  142.4 0.0 copy-done.1
  142.4 0.6 copy.7
Async XLA Ops:
  1.3 1.0 copy-start
  133.5 8.9 %copy-start.1 = (f32[32,128]{1,0:T(8,128)S(1)}, f32[32,128]{1,0:T(8,128)}, u32[]{:S(2)}) copy-start(f32[32,128]{1,0:T(8,128)} %get-tuple-element.7) | copy-start | bytes 49156

commit v4 on v3

--- a/solution.py
+++ b/solution.py
@@ -269,7 +269,7 @@
             slot = turn(k)
             hit = jnp.float32(1e30)
             for l in range(LIST_MAX):
-                same = (slots_ref[kb, l] == slot) & (count > l)
+                same = (lax.div(slots_ref[kb, l], own_blocks) == slot) & (count > l)
                 hit = jnp.where(same, jnp.float32(0.0), hit)
             less[kb, k] = hit
         return c
@@ -613,12 +613,12 @@
             if t == 0:
 
                 def name(j, c):
-                    for u in range(4):
-                        i = j * 4 + u
+                    for u in range(8):
+                        i = j * 8 + u
                         ids[i] = jnp.max(con[i, pl.ds(CBLK + 2, 1), :]).astype(jnp.int32)
                     return c
 
-                lax.fori_loop(h * half // 4, (h + 1) * half // 4, name, 0)
+                lax.fori_loop(h * half // 8, (h + 1) * half // 8, name, 0)
                 if h == 0:
                     book.wait()
 
@@ -802,7 +802,7 @@
                 dma, dma, dma((n_code,)), dma((n,)), dma((ITERS,)),
             ],
             compiler_params=params(collective_id=0, has_side_effects=True),
-        )(slots, counts, want, cached_keys, book)
+        )(block_lists, counts, want, cached_keys, book)
         current = finish(results[:ITERS], book)
         return (current.reshape(own_rows, feature), results[ITERS].reshape(-1))
 

time: 143 us -> 143 us (level)
  no operation moved by 1% of the time
where the time goes in v4:
time: 143 us
  Pallas kernels  140 us (98%)
  local copies, waits for them, and re-layouts  1.47 us (1%)
    pallas_call x1, Pallas kernels, on_device(): pl.pallas_call(functools.partial(sweeps_kernel, n_dp, n_code, key_blocks,...  131 us
    pallas_call x1, Pallas kernels, finish(): pl.pallas_call(functools.partial(finish_kernel, n, own_blocks, len(parts)...  8.66 us

profile of v4, /device:TPU:1, one launch (start us, length us, event | category | flops | bytes accessed | tf_op | source)
XLA Modules:
  0.0 142.8 jit_solution(17690308298963966055)
XLA Ops:
  0.6 0.7 add_select_fusion.1
  1.3 0.1 eq.17
  1.4 0.1 broadcast_in_dim.21
  1.5 0.1 select_reduce_fusion
  1.6 0.7 broadcast_in_dim.24.refs_2_
  2.3 131.2 %shard_map.59 = (f32[32,264,128]{2,1,0:T(8,128)}, f32[32,264,128]{2,1,0:T(8,128)}, f32[32,128]{1,0:T(8,128)}) custom-call(s32[8,6]{1,0:T(8,128)} %refs_0_.1, s32[8]{0:T(128)} %refs_1_.1, s32[8,8,128]{2,1,0:T(8,128)} %broadcast_in_dim.24.refs_2_, bf16[4096,128]{1,0:T(8,128)(2,1)} %refs_3_.1, f32[32,256,128]{2,1,0:T(8,128)} %bitcast.4), custom_call_target="tpu_custom_call" | custom-call | tf_op jit(solution)/shard_map/pallas_call | solution.py:769
  133.5 0.0 copy-start
  133.5 8.7 %shard_map.60 = f32[32,256,128]{2,1,0:T(8,128)} custom-call(f32[32,264,128]{2,1,0:T(8,128)} %get-tuple-element.5.refs_0_, f32[32,264,128]{2,1,0:T(8,128)} %get-tuple-element.6.refs_1_, f32[32,256,128]{2,1,0:T(8,128)} %bitcast.5), custom_call_target="tpu_custom_call" | custom-call | tf_op jit(solution)/shard_map/pallas_call | solution.py:745
  142.2 0.0 copy-done
  142.2 0.6 copy.7
Async XLA Ops:
  133.5 8.7 %copy-start = (f32[32,128]{1,0:T(8,128)S(1)}, f32[32,128]{1,0:T(8,128)}, u32[]{:S(2)}) copy-start(f32[32,128]{1,0:T(8,128)} %get-tuple-element.7) | copy-start | bytes 49156
